TPU v7x, 128 devices: a whole 4x4x4 slice. The times are simulated.
128 devices in a mesh: az: 8 (over z_lo, y), col: 16 (over z_hi, x, core).
Axes of the slice: x: 4, y: 4, z: 4 (z_hi: 2, z_lo: 2; z = z_hi * 2 + z_lo), core: 2. Of those that a mesh axis runs over, the one named last changes fastest.
Arguments:
- phase_field: float32 [64, 1024, 2048], P(None, 'col', 'az'), may hold values from -1 to 1
- velocity: bfloat16 [2, 64, 1024, 2048], P(None, None, 'col', 'az'), may hold values from -4 to 4
- owned_modes: int32 [128, 4], replicated, may hold values from 0 to 511, as said below
- legendre: bfloat16 [512, 1024, 512], P(('az', 'col')), as said below
- radial_inverse: bfloat16 [512, 64, 64], replicated, as said below
Outputs:
- new_phase: float32 [64, 1024, 2048], P(None, 'col', 'az')
Inputs may be any that keep to these rules, and one draw needn't show every extreme that they name: `owned_modes`: every order from 0 to 511 appears exactly once; the second half of each row is 511 minus its first half. legendre[q, t, l] is the orthonormal associated Legendre function of degree l and order m_q (owned_modes flattened at q) at cos(theta_t), normalized so that the integral of its square times sin(theta) over theta is 1, rounded to bfloat16; it is 0 for l < m_q. `radial_inverse`: one matrix for each degree.
All inputs are finite; a program needn't handle non-finite values.
Results may differ from a plain program's by a relative error of at most 0.0003.
Values sent between devices are 32-bit elements; how exact they have to be, the bound alone decides.
No kernel may reach another device: no remote copies, remote signals or barrier semaphores. Data moves between devices by JAX's collectives and lax.ppermute only.
A program may use at most 192 MiB of HBM per device.

v0:
```python
import math
import jax
import jax.numpy as jnp
from jax import lax
from jax.sharding import PartitionSpec as P

step_time = 0.002
mobility_step = 4e-06
highest_precision = lax.Precision.HIGHEST


def padded_2(block, sides, width):
    for axis, dim in sides:
        count = lax.axis_size(axis)
        forward = [(i, i + 1) for i in range(count - 1)]
        forward.append((count - 1, 0))
        backward = [(target, source) for source, target in forward]
        low = lax.ppermute(
            lax.slice_in_dim(block, block.shape[dim] - width, None, axis=dim), axis, forward
        )
        high = lax.ppermute(lax.slice_in_dim(block, 0, width, axis=dim), axis, backward)
        block = jnp.concatenate([low, block, high], axis=dim)
    return block


def shell_radii(shells):
    return 0.75 + 0.25 * (jnp.arange(shells, dtype=jnp.float32) + 0.5) / shells


def colat_weights(count):
    row_index = jnp.arange(count, dtype=jnp.int32)
    waves = jnp.arange(1, count // 2 + 1, dtype=jnp.int32)
    turns = (2 * row_index[:, None] + 1) * waves[None, :] % (2 * count)
    cosines = jnp.cos(turns.astype(jnp.float32) * (math.pi / count))
    wave_float = waves.astype(jnp.float32)
    coefs = 1.0 / (4.0 * wave_float * wave_float - 1.0)
    return 2.0 / count * (1.0 - 2.0 * jnp.dot(cosines, coefs, precision=highest_precision))


def forward_waves(phi_index, mode_list, phi_count):
    turns = phi_index[:, None] * mode_list[None, :] % phi_count
    angle = turns.astype(jnp.float32) * (2.0 * math.pi / phi_count)
    return jnp.stack([jnp.cos(angle), -jnp.sin(angle)], axis=1) / phi_count


def inverse_waves(mode_list, phi_count):
    phi_index = jnp.arange(phi_count, dtype=jnp.int32)
    turns = mode_list[:, None] * phi_index[None, :] % phi_count
    angle = turns.astype(jnp.float32) * (2.0 * math.pi / phi_count)
    doubling = jnp.where(mode_list == 0, 1.0, 2.0).astype(jnp.float32)[:, None]
    return jnp.stack([doubling * jnp.cos(angle), -doubling * jnp.sin(angle)], axis=0)


def body(phase_field, velocity, owned_modes, legendre, radial_inverse):
    shells, theta_local, phi_local = phase_field.shape
    az_count = lax.axis_size("az")
    col_count = lax.axis_size("col")
    phi_count = phi_local * az_count
    theta_count = theta_local * col_count
    theta_block = theta_local // az_count
    mode_list = owned_modes.reshape(-1)
    mode_count = mode_list.shape[0]
    mode_dev = legendre.shape[0]
    degree_count = legendre.shape[2]
    legendre_full = legendre.astype(jnp.float32)
    shell_radius = shell_radii(shells)
    padded = padded_2(phase_field, (("az", 2), ("col", 1)), 1)
    col_here = lax.axis_index("col")
    row_index = jnp.arange(theta_local + 2, dtype=jnp.int32)
    row_mask = jnp.logical_not(
        jnp.logical_or(
            jnp.logical_and(row_index == 0, col_here == 0),
            jnp.logical_and(row_index == theta_local + 1, col_here == col_count - 1),
        )
    )
    padded = padded * row_mask.astype(jnp.float32)[None, :, None]
    centre_rows = padded[:, 1:-1, :]
    east_cell = centre_rows[:, :, 2:]
    west_cell = centre_rows[:, :, :-2]
    south_cell = padded[:, 2:, 1:-1]
    north_cell = padded[:, :-2, 1:-1]
    d_phi = (east_cell - west_cell) * (phi_count / (4.0 * math.pi))
    d_theta = (south_cell - north_cell) * (theta_count / (2.0 * math.pi))
    spin_rate = velocity[0].astype(jnp.float32)
    sweep_speed = velocity[1].astype(jnp.float32)
    advected = phase_field - step_time * (
        spin_rate * d_phi + sweep_speed / shell_radius[:, None, None] * d_theta
    )
    potential = phase_field * phase_field * phase_field - phase_field
    fields = jnp.stack([advected, potential])
    wave_table = forward_waves(jnp.arange(phi_count, dtype=jnp.int32), mode_list, phi_count)
    spectra = jnp.einsum(
        "frtp,pqk->ktqfr",
        lax.all_to_all(fields, "az", split_axis=2, concat_axis=3, tiled=True),
        wave_table,
        precision=highest_precision,
    )
    spectra = spectra.reshape(mode_count, theta_block, 4 * shells)
    gathered = lax.all_to_all(spectra, ("az", "col"), split_axis=0, concat_axis=1, tiled=True)
    gathered = gathered.reshape(mode_dev, az_count, col_count, theta_block, 4 * shells)
    gathered = jnp.transpose(gathered, (0, 2, 1, 3, 4))
    gathered = gathered.reshape(mode_dev, theta_count, 4 * shells)
    weights = colat_weights(theta_count)
    weighted = gathered * weights[None, :, None]
    coeffs = jnp.einsum("ktx,ktl->klx", weighted, legendre_full, precision=highest_precision)
    coeffs = coeffs.reshape(mode_dev, degree_count, 2, 2, shells)
    degrees = jnp.arange(degree_count, dtype=jnp.float32)
    factor = (
        mobility_step
        * (degrees * (degrees + 1.0))[:, None]
        / (shell_radius * shell_radius)[None, :]
    )
    right_side = coeffs[:, :, :, 0, :] - factor[None, :, None, :] * coeffs[:, :, :, 1, :]
    solved = jnp.einsum(
        "lrs,klqs->klqr",
        radial_inverse.astype(jnp.float32),
        right_side,
        precision=highest_precision,
    )
    synthesis = jnp.einsum(
        "ktl,klx->ktx",
        legendre_full,
        solved.reshape(mode_dev, degree_count, 2 * shells),
        precision=highest_precision,
    )
    synthesis = synthesis.reshape(mode_dev, col_count, az_count, theta_block, 2 * shells)
    synthesis = jnp.transpose(synthesis, (0, 2, 1, 3, 4)).reshape(mode_dev, theta_count, 2 * shells)
    grid_modes = lax.all_to_all(synthesis, ("az", "col"), split_axis=1, concat_axis=0, tiled=True)
    grid_modes = grid_modes.reshape(mode_count, theta_block, 2, shells)
    inverse_table = inverse_waves(mode_list, phi_count)
    row_fields = jnp.einsum("ktqr,qkp->rtp", grid_modes, inverse_table, precision=highest_precision)
    new_phase = lax.all_to_all(row_fields, "az", split_axis=2, concat_axis=1, tiled=True)
    return new_phase


def solution(mesh):
    in_specs = (
        P(None, "col", "az"),
        P(None, None, "col", "az"),
        P(),
        P(("az", "col"), None, None),
        P(),
    )
    out_specs = P(None, "col", "az")
    return jax.shard_map(body, mesh=mesh, in_specs=in_specs, out_specs=out_specs, check_vma=False)
```

profile of v0, /device:TPU:0, one launch (start us, length us, event | category | flops | bytes accessed | tf_op | source)
XLA Modules:
  0.0 518.3 jit_solution(17031054977183519346)
XLA Ops:
  27.1 5.6 %collective-permute-start.3 = (f32[64,1,258]{2,0,1:T(8,128)S(1)}, f32[64,1,258]{2,0,1:T(8,128)S(1)}, u32[]{:S(2)}, u32[]{:S(2)}) collective-permute-start(f32[64,1,258]{2,0,1:T(8,128)S(1)} %get-tuple-element.6), channel_id=1, source_target_pairs={{1,0},{2,1},{3,2},{4,3},{5,4},{6,5},{7,6},{8,7},{9,8},{10,9},{11,1... | collective-permute-start | bytes 198152 | tf_op jit(solution)/shard_map/ppermute | solution.py:21
  38.1 10.6 %fusion.20 = (f32[1,64,64,256]{3,1,0,2:T(8,128)S(1)}, f32[1,64,64,256]{3,1,0,2:T(8,128)}) fusion(f32[64,66,258]{2,0,1:T(8,128)S(1)} %maximum_multiply_fusion.1, bf16[1,64,64,256]{3,2,1,0:T(8,128)(2,1)} %get-tuple-element.10, bf16[1,64,64,256]{3,2,1,0:T(8,128)(2,1)} %get-tuple-element.9, f32[64]{0:T(128)S(1)} %multiply_add_fusion.1, ...), kind=kLoop, calls=%fused_computation.32 | loop fusion | flops 15728640 | bytes 33554688 | tf_op jit(solution)/shard_map/stack | solution.py:90
  48.7 6.3 %pad_maximum_fusion = f32[2,64,64,256]{3,1,0,2:T(8,128)} fusion(f32[1,64,64,256]{3,1,0,2:T(8,128)} %get-tuple-element.8, f32[1,64,64,256]{3,1,0,2:T(8,128)S(1)} %get-tuple-element.7), kind=kLoop, calls=%fused_computation.9 | loop fusion | flops 2097152 | bytes 16777216 | tf_op jit(solution)/shard_map/stack | solution.py:90
  60.8 18.0 %fusion.47 = (f32[2048,1,512]{2,0,1:T(8,128)}, f32[2048,1,512]{2,0,1:T(8,128)}) fusion(s32[512]{0:T(512)S(1)} %reshape.391), kind=kLoop, calls=%fused_computation.68 | loop fusion | flops 15728640 | bytes 8390656 | tf_op jit(solution)/shard_map/cos | solution.py:43
  78.9 75.0 %all-to-all-done = f32[2,64,64,256]{3,1,0,2:T(8,128)} async-done(((f32[2,64,64,256]{3,1,0,2:T(8,128)}), f32[2,64,64,256]{3,1,0,2:T(8,128)}, u32[]{:S(2)}, u32[]{:S(2)}) %all-to-all-start) | async-done | bytes 8388640 | tf_op jit(solution)/shard_map/all_to_all | solution.py:94
  153.8 13.2 %copy.100 = f32[2,64,8,8,256]{4,2,1,3,0:T(8,128)} copy(f32[2,64,8,8,256]{4,1,0,3,2:T(8,128)} %bitcast.6) | data formatting | bytes 16777216 | tf_op jit(solution)/shard_map/all_to_all | solution.py:94
  167.0 9.3 %reshape.403 = f32[2,64,8,2048,1]{3,1,2,0,4:T(8,128)} reshape(f32[2,64,8,8,256]{4,3,1,2,0:T(8,128)} %bitcast.103) | data formatting | bytes 16777216 | tf_op jit(solution)/shard_map/all_to_all | solution.py:94
  176.3 32.7 %fusion.34 = f32[512,8,2,2,64]{0,4,1,3,2:T(8,128)S(1)} fusion(f32[2,64,8,2048,1]{3,1,2,0,4:T(8,128)} %reshape.403, f32[2048,1,512]{2,0,1:T(8,128)} %get-tuple-element.20, f32[2048,1,512]{2,0,1:T(8,128)} %get-tuple-element.19), kind=kOutput, calls=%fused_computation.55 | convolution fusion | flops 25773998080 | bytes 20971520 | tf_op jit(solution)/shard_map/frtp,pqk->ktqfr/dot_general | solution.py:92
  217.0 40.8 %all-to-all-start.1 = ((f32[512,8,256]{2,1,0:T(8,128)}), f32[512,8,256]{2,1,0:T(8,128)}, u32[]{:S(2)}, u32[]{:S(2)}) async-start(f32[512,8,256]{2,1,0:T(8,128)} %copy.57), calls=%async_computation.1 | async-start | bytes 8388608 | tf_op jit(solution)/shard_map/all_to_all | solution.py:99
  257.8 13.0 %copy.75 = bf16[512,64,64,1]{2,1,3,0:T(8,128)(2,1)} copy(bf16[512,64,64,1]{0,2,1,3:T(8,128)(2,1)} %bitcast.109) | data formatting | bytes 8388608 | tf_op args[4]
  270.8 9.9 %fusion.40 = f32[1,1024]{1,0:T(1,128)S(1)} fusion(f32[512,1]{0,1:T(1,128)S(1)} %bitcast.112, s32[512]{0:T(512)S(1)} %iota_add_fusion, s32[1024]{0:T(1024)S(1)} %multiply_add_fusion), kind=kOutput, calls=%fused_computation.59 | convolution fusion | flops 13631488 | bytes 12288 | tf_op jit(solution)/shard_map/dot_general | solution.py:37
  280.9 29.5 %all-to-all-done.1 = f32[512,8,256]{2,1,0:T(8,128)} async-done(((f32[512,8,256]{2,1,0:T(8,128)}), f32[512,8,256]{2,1,0:T(8,128)}, u32[]{:S(2)}, u32[]{:S(2)}) %all-to-all-start.1) | async-done | bytes 4194336 | tf_op jit(solution)/shard_map/all_to_all | solution.py:99
  323.8 17.1 %fusion.51 = f32[4,512,2,64]{3,0,2,1:T(4,128)} fusion(bf16[512,64,64,1]{2,1,3,0:T(8,128)(2,1)} %copy.75, f32[4,512,2,1,64]{4,0,2,1,3:T(4,128)} %copy.85, f32[4,512,2,1,64]{4,0,2,1,3:T(4,128)S(1)} %copy.84, f32[512,64]{1,0:T(8,128)S(1)} %broadcast_divide_fusion), kind=kOutput, calls=%fused_computation.73 | convolution fusion | flops 201850880 | bytes 7471104 | tf_op jit(solution)/shard_map/lrs,klqs->klqr/dot_general | solution.py:114
  342.8 6.4 %convolution_bitcast_fusion = f32[4,1024,128]{1,2,0:T(8,128)S(1)} fusion(f32[4,512,128]{1,2,0:T(8,128)S(1)} %bitcast.110, bf16[4,1024,512]{2,1,0:T(8,128)(2,1)} %param.8), kind=kOutput, calls=%fused_computation.72 | convolution fusion | flops 3221225472 | bytes 7340032 | tf_op jit(solution)/shard_map/ktl,klx->ktx/dot_general | solution.py:120
  355.5 5.8 %all-to-all-start.2 = ((f32[4,1024,128]{2,0,1:T(4,128)}), f32[4,1024,128]{2,0,1:T(4,128)S(1)}, u32[]{:S(2)}, u32[]{:S(2)}) async-start(f32[4,1024,128]{2,0,1:T(4,128)} %copy.67), calls=%async_computation.2 | async-start | bytes 4194304 | tf_op jit(solution)/shard_map/all_to_all | solution.py:128
  361.3 19.1 %cosine_multiply_fusion = (f32[1,512,2048]{2,1,0:T(8,128)}, f32[1,512,2048]{2,1,0:T(8,128)}) fusion(s32[512]{0:T(512)S(1)} %reshape.391, f32[512]{0:T(512)S(1)} %get-tuple-element.17, f32[512]{0:T(512)S(1)} %get-tuple-element.18), kind=kLoop, calls=%fused_computation.44 | loop fusion | flops 16777216 | bytes 8394752 | tf_op jit(solution)/shard_map/mul | solution.py:51
  380.4 11.3 %all-to-all-done.2 = f32[4,1024,128]{2,0,1:T(4,128)S(1)} async-done(((f32[4,1024,128]{2,0,1:T(4,128)}), f32[4,1024,128]{2,0,1:T(4,128)S(1)}, u32[]{:S(2)}, u32[]{:S(2)}) %all-to-all-start.2) | async-done | bytes 2097184 | tf_op jit(solution)/shard_map/all_to_all | solution.py:128
  395.8 21.0 %fusion.31 = f32[64,8,2048]{2,0,1:T(8,128)} fusion(f32[512,8,2,64]{3,2,1,0:T(2,128)} %reshape.399, f32[1,512,2048]{2,1,0:T(8,128)} %get-tuple-element.16, f32[1,512,2048]{2,1,0:T(8,128)} %get-tuple-element.15), kind=kOutput, calls=%fused_computation.52 | convolution fusion | flops 12886999040 | bytes 14680064 | tf_op jit(solution)/shard_map/ktqr,qkp->rtp/dot_general | solution.py:131
  416.8 7.0 %copy.71 = f32[64,8,2048]{0,1,2:T(8,128)} copy(f32[64,8,2048]{2,0,1:T(8,128)} %fusion.31) | data formatting | bytes 8388608 | tf_op jit(solution)/shard_map/ktqr,qkp->rtp/transpose | solution.py:131
  423.8 10.0 %reshape.410 = f32[8,1,131072]{2,1,0:T(1,128)} reshape(f32[2048,8,64]{2,1,0:T(8,128)} %bitcast.101) | data formatting | bytes 8388608
  433.8 53.7 %all_to_all.66 = f32[8,1,131072]{2,1,0:T(1,128)} all-to-all(f32[8,1,131072]{2,1,0:T(1,128)} %reshape.410), channel_id=1, replica_groups=mesh['az'=8,'col'=16] {'az'}, dimensions={0} | all-to-all | bytes 8388608 | tf_op jit(solution)/shard_map/all_to_all | solution.py:132
  488.1 13.8 %reduce = f32[8,131072]{1,0:T(8,128)} reduce(f32[8,1,131072]{2,1,0:T(1,128)} %all_to_all.66, f32[]{:T(128)} %broadcast.379), dimensions={1}, to_apply=%all_to_all.58.reduce_sub_computation | reduce | bytes 8388612 | tf_op jit(solution)/shard_map/all_to_all | solution.py:132
  501.8 8.7 %reshape.411 = f32[2048,8,64]{2,1,0:T(8,128)} reshape(f32[8,131072]{1,0:T(8,128)} %reduce) | data formatting | bytes 8388608
  510.5 7.6 %copy.72 = f32[64,8,8,256]{3,2,1,0:T(8,128)} copy(f32[64,8,8,256]{0,2,3,1:T(8,128)} %bitcast.102) | data formatting | bytes 8388608 | tf_op jit(solution)/shard_map/all_to_all | solution.py:132
  (57 shorter events, 72.6 us)
Async XLA Ops:
  6.5 14.5 %collective-permute-start = (f32[64,64,1]{1,0,2:T(8,128)S(1)}, f32[64,64,1]{1,0,2:T(8,128)S(1)}, u32[]{:S(2)}, u32[]{:S(2)}) collective-permute-start(f32[64,64,1]{1,0,2:T(8,128)S(1)} %copy.81), channel_id=1, source_target_pairs={{0,16},{16,32},{32,48},{48,64},{64,80},{80,96},{96,112},{112,0},{1... | collective-permute-start | bytes 49160 | tf_op jit(solution)/shard_map/ppermute | solution.py:18
  8.9 7.6 %copy-start = (f32[64,64,256]{2,1,0:T(8,128)S(1)}, f32[64,64,256]{2,1,0:T(8,128)}, u32[]{:S(2)}) copy-start(f32[64,64,256]{2,1,0:T(8,128)} %param.5) | copy-start | bytes 12582916
  8.9 14.0 %collective-permute-start.1 = (f32[64,64,1]{1,0,2:T(8,128)S(1)}, f32[64,64,1]{1,0,2:T(8,128)S(1)}, u32[]{:S(2)}, u32[]{:S(2)}) collective-permute-start(f32[64,64,1]{1,0,2:T(8,128)S(1)} %copy.82), channel_id=1, source_target_pairs={{16,0},{32,16},{48,32},{64,48},{80,64},{96,80},{112,96},{0,112},{1... | collective-permute-start | bytes 49160 | tf_op jit(solution)/shard_map/ppermute | solution.py:21
  25.8 9.1 %copy-start.2 = (f32[64,64,256]{2,0,1:T(8,128)S(1)}, f32[64,64,256]{2,0,1:T(8,128)}, u32[]{:S(2)}) copy-start(f32[64,64,256]{2,0,1:T(8,128)} %copy.50) | copy-start | bytes 12582916
  25.8 9.1 %copy-start.3 = (f32[64,64,1]{2,0,1:T(8,128)S(1)}, f32[64,64,1]{2,0,1:T(8,128)}, u32[]{:S(2)}) copy-start(f32[64,64,1]{2,0,1:T(8,128)} %copy.48) | copy-start | bytes 49156
  27.0 7.7 %collective-permute-start.2 = (f32[64,1,258]{2,0,1:T(8,128)S(1)}, f32[64,1,258]{2,0,1:T(8,128)S(1)}, u32[]{:S(2)}, u32[]{:S(2)}) collective-permute-start(f32[64,1,258]{2,0,1:T(8,128)S(1)} %get-tuple-element.5), channel_id=1, source_target_pairs={{0,1},{1,2},{2,3},{3,4},{4,5},{5,6},{6,7},{7,8},{8,9},{9,10},{10,1... | collective-permute-start | bytes 198152 | tf_op jit(solution)/shard_map/ppermute | solution.py:18
  27.1 7.8 %collective-permute-start.3 = (f32[64,1,258]{2,0,1:T(8,128)S(1)}, f32[64,1,258]{2,0,1:T(8,128)S(1)}, u32[]{:S(2)}, u32[]{:S(2)}) collective-permute-start(f32[64,1,258]{2,0,1:T(8,128)S(1)} %get-tuple-element.6), channel_id=1, source_target_pairs={{1,0},{2,1},{3,2},{4,3},{5,4},{6,5},{7,6},{8,7},{9,8},{10,9},{11,1... | collective-permute-start | bytes 198152 | tf_op jit(solution)/shard_map/ppermute | solution.py:21
  32.7 5.4 %copy-start.1 = (f32[64,64,256]{2,1,0:T(8,128)S(1)}, f32[64,64,256]{2,1,0:T(8,128)}, u32[]{:S(2)}) copy-start(f32[64,64,256]{2,1,0:T(8,128)} %param.5) | copy-start | bytes 12582916
  55.0 5.6 %copy-start.5 = (s32[128,4]{0,1:T(4,128)S(1)}, s32[128,4]{0,1:T(4,128)}, u32[]{:S(2)}) copy-start(s32[128,4]{0,1:T(4,128)} %param.7) | copy-start | bytes 6148
  55.0 98.8 %all-to-all-start = ((f32[2,64,64,256]{3,1,0,2:T(8,128)}), f32[2,64,64,256]{3,1,0,2:T(8,128)}, u32[]{:S(2)}, u32[]{:S(2)}) async-start(f32[2,64,64,256]{3,1,0,2:T(8,128)} %pad_maximum_fusion), calls=%async_computation | async-start | bytes 16777216 | tf_op jit(solution)/shard_map/all_to_all | solution.py:94
  217.0 93.4 %all-to-all-start.1 = ((f32[512,8,256]{2,1,0:T(8,128)}), f32[512,8,256]{2,1,0:T(8,128)}, u32[]{:S(2)}, u32[]{:S(2)}) async-start(f32[512,8,256]{2,1,0:T(8,128)} %copy.57), calls=%async_computation.1 | async-start | bytes 8388608 | tf_op jit(solution)/shard_map/all_to_all | solution.py:99
  313.1 2.2 copy-start.4
  355.5 36.2 %all-to-all-start.2 = ((f32[4,1024,128]{2,0,1:T(4,128)}), f32[4,1024,128]{2,0,1:T(4,128)S(1)}, u32[]{:S(2)}, u32[]{:S(2)}) async-start(f32[4,1024,128]{2,0,1:T(4,128)} %copy.67), calls=%async_computation.2 | async-start | bytes 4194304 | tf_op jit(solution)/shard_map/all_to_all | solution.py:128
where the time goes:
time: 526 us; the launch traced here: 518 us
  local copies, waits for them, and re-layouts  120 us (23%)
  waiting for transfers between devices  118 us (22%)
  matrix products  90.6 us (17%)
  other arithmetic  73 us (14%)
  starting transfers between devices  62.4 us (12%)
  blocking collectives  53.7 us (10%)
    all_to_all x1, waiting for transfers between devices, body(): lax.all_to_all(fields, 'az', split_axis=2, concat_axis=3, tiled=True)  75 us
    all_to_all x1, blocking collectives, body(): lax.all_to_all(row_fields, 'az', split_axis=2, concat_axis=1, tiled=True)  53.7 us
    unnamed x21, local copies, waits for them, and re-layouts  44.6 us
    all_to_all x1, starting transfers between devices, body(): lax.all_to_all(spectra, ('az', 'col'), split_axis=0, concat_axis=1, tiled...  40.8 us
    dot_general x1, matrix products, body(): jnp.einsum('frtp,pqk->ktqfr', lax.all_to_all(fields, 'az', split_axis=2,...  32.7 us
    all_to_all x1, waiting for transfers between devices, body(): lax.all_to_all(spectra, ('az', 'col'), split_axis=0, concat_axis=1, tiled...  29.5 us
    all_to_all x2, local copies, waits for them, and re-layouts, body(): lax.all_to_all(fields, 'az', split_axis=2, concat_axis=3, tiled=True)  22.5 us
    dot_general x1, matrix products, body(): jnp.einsum('ktqr,qkp->rtp', grid_modes, inverse_table, precision=highest_...  21 us
  transfers between devices with their start and end apart: 7, of which 5 were waited for; matrix products, arithmetic and copies ran while one was open for 14% of the time, Pallas kernels for 0%

commit v1 on v0

--- a/solution.py
+++ b/solution.py
@@ -129,7 +129,15 @@
     grid_modes = grid_modes.reshape(mode_count, theta_block, 2, shells)
     inverse_table = inverse_waves(mode_list, phi_count)
     row_fields = jnp.einsum("ktqr,qkp->rtp", grid_modes, inverse_table, precision=highest_precision)
-    new_phase = lax.all_to_all(row_fields, "az", split_axis=2, concat_axis=1, tiled=True)
+    new_phase = jnp.concatenate(
+        lax.all_to_all(
+            jnp.stack(jnp.split(row_fields, lax.axis_size("az"), axis=2), axis=0),
+            "az",
+            split_axis=0,
+            concat_axis=0,
+        ),
+        axis=1,
+    )
     return new_phase
 
 

time: 526 us -> 480 us (0.913)
  local copies, waits for them, and re-layouts: 120 us -> 91.2 us
  other arithmetic: 73 us -> 59.2 us
    unnamed x21 -> x26, local copies, waits for them, and re-layouts: 44.6 us -> 26.2 us
    all_to_all x1 -> x0, other arithmetic: 13.8 us -> none  [body(): lax.all_to_all(row_fields, 'az', split_axis=2, concat_axis=1, tiled=True)]
    all_to_all x2 -> x0, local copies, waits for them, and re-layouts: 8.14 us -> none  [body(): lax.all_to_all(row_fields, 'az', split_axis=2, concat_axis=1, tiled=True)]
    transpose x1 -> x0, local copies, waits for them, and re-layouts: 6.98 us -> none  [body(): jnp.einsum('ktqr,qkp->rtp', grid_modes, inverse_table, precision=highest_...]
  transfers between devices with their start and end apart: 7 -> 7, of which waited for: 5 -> 5; matrix products, arithmetic and copies ran while one was open for 14% -> 15% of each run, Pallas kernels for 0% -> 0%
where the time goes in v1:
time: 480 us; the launch traced here: 473 us
  waiting for transfers between devices  118 us (25%)
  local copies, waits for them, and re-layouts  91.2 us (19%)
  matrix products  89.5 us (19%)
  starting transfers between devices  62.2 us (13%)
  other arithmetic  59.2 us (12%)
  blocking collectives  52.2 us (11%)
    all_to_all x1, waiting for transfers between devices, body(): lax.all_to_all(fields, 'az', split_axis=2, concat_axis=3, tiled=True)  75 us
    all_to_all x1, blocking collectives, body(): lax.all_to_all(jnp.stack(jnp.split(row_fields, lax.axis_size('az'), axis=...  52.2 us
    all_to_all x1, starting transfers between devices, body(): lax.all_to_all(spectra, ('az', 'col'), split_axis=0, concat_axis=1, tiled...  40.7 us
    dot_general x1, matrix products, body(): jnp.einsum('frtp,pqk->ktqfr', lax.all_to_all(fields, 'az', split_axis=2,...  33.1 us
    all_to_all x1, waiting for transfers between devices, body(): lax.all_to_all(spectra, ('az', 'col'), split_axis=0, concat_axis=1, tiled...  29.5 us
    unnamed x26, local copies, waits for them, and re-layouts  26.2 us
    all_to_all x2, local copies, waits for them, and re-layouts, body(): lax.all_to_all(fields, 'az', split_axis=2, concat_axis=3, tiled=True)  22.5 us
    dot_general x1, matrix products, body(): jnp.einsum('ktqr,qkp->rtp', grid_modes, inverse_table, precision=highest_...  19.7 us
  transfers between devices with their start and end apart: 7, of which 5 were waited for; matrix products, arithmetic and copies ran while one was open for 15% of the time, Pallas kernels for 0%

profile of v1, /device:TPU:0, one launch (start us, length us, event | category | flops | bytes accessed | tf_op | source)
XLA Modules:
  0.0 472.6 jit_solution(7304477396417364079)
XLA Ops:
  11.7 4.7 %fusion.81 = (bf16[1,64,64,256]{3,2,1,0:T(8,128)(2,1)}, bf16[1,64,64,256]{3,2,1,0:T(8,128)(2,1)}) fusion(bf16[2,64,64,256]{3,2,1,0:T(8,128)(2,1)} %param.6), kind=kLoop, calls=%fused_computation.121 | loop fusion | bytes 8388608 | tf_op jit(solution)/shard_map/slice | solution.py:84
  16.5 4.4 copy.50
  27.1 5.6 %collective-permute-start.3 = (f32[64,1,258]{2,0,1:T(8,128)S(1)}, f32[64,1,258]{2,0,1:T(8,128)S(1)}, u32[]{:S(2)}, u32[]{:S(2)}) collective-permute-start(f32[64,1,258]{2,0,1:T(8,128)S(1)} %get-tuple-element.6), channel_id=1, source_target_pairs={{1,0},{2,1},{3,2},{4,3},{5,4},{6,5},{7,6},{8,7},{9,8},{10,9},{11,1... | collective-permute-start | bytes 198152 | tf_op jit(solution)/shard_map/ppermute | solution.py:21
  38.0 10.6 %fusion.20 = (f32[1,64,64,256]{3,1,0,2:T(8,128)S(1)}, f32[1,64,64,256]{3,1,0,2:T(8,128)}) fusion(f32[64,66,258]{2,0,1:T(8,128)S(1)} %maximum_multiply_fusion.1, bf16[1,64,64,256]{3,2,1,0:T(8,128)(2,1)} %get-tuple-element.10, bf16[1,64,64,256]{3,2,1,0:T(8,128)(2,1)} %get-tuple-element.9, f32[64]{0:T(128)S(1)} %multiply_add_fusion.1, ...), kind=kLoop, calls=%fused_computation.32 | loop fusion | flops 15728640 | bytes 33554688 | tf_op jit(solution)/shard_map/stack | solution.py:90
  48.7 6.2 %pad_maximum_fusion = f32[2,64,64,256]{3,1,0,2:T(8,128)} fusion(f32[1,64,64,256]{3,1,0,2:T(8,128)} %get-tuple-element.8, f32[1,64,64,256]{3,1,0,2:T(8,128)S(1)} %get-tuple-element.7), kind=kLoop, calls=%fused_computation.9 | loop fusion | flops 2097152 | bytes 16777216 | tf_op jit(solution)/shard_map/stack | solution.py:90
  54.9 5.4 %all-to-all-start = ((f32[2,64,64,256]{3,1,0,2:T(8,128)}), f32[2,64,64,256]{3,1,0,2:T(8,128)}, u32[]{:S(2)}, u32[]{:S(2)}) async-start(f32[2,64,64,256]{3,1,0,2:T(8,128)} %pad_maximum_fusion), calls=%async_computation | async-start | bytes 16777216 | tf_op jit(solution)/shard_map/all_to_all | solution.py:94
  60.6 18.0 %fusion.47 = (f32[2048,1,512]{2,0,1:T(8,128)}, f32[2048,1,512]{2,0,1:T(8,128)}) fusion(s32[512]{0:T(512)S(1)} %reshape.397), kind=kLoop, calls=%fused_computation.68 | loop fusion | flops 15728640 | bytes 8390656 | tf_op jit(solution)/shard_map/cos | solution.py:43
  78.6 75.0 %all-to-all-done = f32[2,64,64,256]{3,1,0,2:T(8,128)} async-done(((f32[2,64,64,256]{3,1,0,2:T(8,128)}), f32[2,64,64,256]{3,1,0,2:T(8,128)}, u32[]{:S(2)}, u32[]{:S(2)}) %all-to-all-start) | async-done | bytes 8388640 | tf_op jit(solution)/shard_map/all_to_all | solution.py:94
  153.5 13.2 %copy.99 = f32[2,64,8,8,256]{4,2,1,3,0:T(8,128)} copy(f32[2,64,8,8,256]{4,1,0,3,2:T(8,128)} %bitcast.6) | data formatting | bytes 16777216 | tf_op jit(solution)/shard_map/all_to_all | solution.py:94
  166.7 9.3 %reshape.411 = f32[2,64,8,2048,1]{3,1,2,0,4:T(8,128)} reshape(f32[2,64,8,8,256]{4,3,1,2,0:T(8,128)} %bitcast.130) | data formatting | bytes 16777216 | tf_op jit(solution)/shard_map/all_to_all | solution.py:94
  176.1 33.1 %fusion.34 = f32[512,8,2,2,64]{0,4,1,3,2:T(8,128)S(1)} fusion(f32[2,64,8,2048,1]{3,1,2,0,4:T(8,128)} %reshape.411, f32[2048,1,512]{2,0,1:T(8,128)} %get-tuple-element.20, f32[2048,1,512]{2,0,1:T(8,128)} %get-tuple-element.19), kind=kOutput, calls=%fused_computation.55 | convolution fusion | flops 25773998080 | bytes 20971520 | tf_op jit(solution)/shard_map/frtp,pqk->ktqfr/dot_general | solution.py:92
  211.6 5.4 %copy.57 = f32[512,8,256]{2,1,0:T(8,128)} copy(f32[512,8,256]{0,2,1:T(8,128)} %bitcast.131) | data formatting | bytes 8388608 | tf_op jit(solution)/shard_map/reshape | solution.py:98
  217.0 40.7 %all-to-all-start.1 = ((f32[512,8,256]{2,1,0:T(8,128)}), f32[512,8,256]{2,1,0:T(8,128)}, u32[]{:S(2)}, u32[]{:S(2)}) async-start(f32[512,8,256]{2,1,0:T(8,128)} %copy.57), calls=%async_computation.1 | async-start | bytes 8388608 | tf_op jit(solution)/shard_map/all_to_all | solution.py:99
  257.8 13.0 %copy.74 = bf16[512,64,64,1]{2,1,3,0:T(8,128)(2,1)} copy(bf16[512,64,64,1]{0,2,1,3:T(8,128)(2,1)} %bitcast.137) | data formatting | bytes 8388608 | tf_op args[4]
  270.8 9.9 %fusion.40 = f32[1,1024]{1,0:T(1,128)S(1)} fusion(f32[512,1]{0,1:T(1,128)S(1)} %bitcast.140, s32[512]{0:T(512)S(1)} %iota_add_fusion, s32[1024]{0:T(1024)S(1)} %multiply_add_fusion), kind=kOutput, calls=%fused_computation.59 | convolution fusion | flops 13631488 | bytes 12288 | tf_op jit(solution)/shard_map/dot_general | solution.py:37
  280.9 29.5 %all-to-all-done.1 = f32[512,8,256]{2,1,0:T(8,128)} async-done(((f32[512,8,256]{2,1,0:T(8,128)}), f32[512,8,256]{2,1,0:T(8,128)}, u32[]{:S(2)}, u32[]{:S(2)}) %all-to-all-start.1) | async-done | bytes 4194336 | tf_op jit(solution)/shard_map/all_to_all | solution.py:99
  323.8 16.9 %fusion.51 = f32[4,512,2,64]{3,0,2,1:T(4,128)} fusion(bf16[512,64,64,1]{2,1,3,0:T(8,128)(2,1)} %copy.74, f32[4,512,2,1,64]{4,0,2,1,3:T(4,128)} %copy.84, f32[4,512,2,1,64]{4,0,2,1,3:T(4,128)S(1)} %copy.83, f32[512,64]{1,0:T(8,128)S(1)} %broadcast_divide_fusion), kind=kOutput, calls=%fused_computation.73 | convolution fusion | flops 201850880 | bytes 7471104 | tf_op jit(solution)/shard_map/lrs,klqs->klqr/dot_general | solution.py:114
  342.6 6.4 %convolution_bitcast_fusion = f32[4,1024,128]{1,2,0:T(8,128)S(1)} fusion(f32[4,512,128]{1,2,0:T(8,128)S(1)} %bitcast.138, bf16[4,1024,512]{2,1,0:T(8,128)(2,1)} %param.8), kind=kOutput, calls=%fused_computation.72 | convolution fusion | flops 3221225472 | bytes 7340032 | tf_op jit(solution)/shard_map/ktl,klx->ktx/dot_general | solution.py:120
  355.3 5.8 %all-to-all-start.2 = ((f32[4,1024,128]{2,0,1:T(4,128)}), f32[4,1024,128]{2,0,1:T(4,128)S(1)}, u32[]{:S(2)}, u32[]{:S(2)}) async-start(f32[4,1024,128]{2,0,1:T(4,128)} %copy.67), calls=%async_computation.2 | async-start | bytes 4194304 | tf_op jit(solution)/shard_map/all_to_all | solution.py:128
  361.2 19.1 %cosine_multiply_fusion = (f32[1,512,2048]{2,1,0:T(8,128)}, f32[1,512,2048]{2,1,0:T(8,128)}) fusion(s32[512]{0:T(512)S(1)} %reshape.397, f32[512]{0:T(512)S(1)} %get-tuple-element.17, f32[512]{0:T(512)S(1)} %get-tuple-element.18), kind=kLoop, calls=%fused_computation.44 | loop fusion | flops 16777216 | bytes 8394752 | tf_op jit(solution)/shard_map/mul | solution.py:51
  380.3 11.3 %all-to-all-done.2 = f32[4,1024,128]{2,0,1:T(4,128)S(1)} async-done(((f32[4,1024,128]{2,0,1:T(4,128)}), f32[4,1024,128]{2,0,1:T(4,128)S(1)}, u32[]{:S(2)}, u32[]{:S(2)}) %all-to-all-start.2) | async-done | bytes 2097184 | tf_op jit(solution)/shard_map/all_to_all | solution.py:128
  395.7 19.7 %fusion.31 = f32[64,8,2048]{2,0,1:T(8,128)S(1)} fusion(f32[512,8,2,64]{3,2,1,0:T(2,128)} %reshape.405, f32[1,512,2048]{2,1,0:T(8,128)} %get-tuple-element.16, f32[1,512,2048]{2,1,0:T(8,128)} %get-tuple-element.15), kind=kOutput, calls=%fused_computation.52 | convolution fusion | flops 12886999040 | bytes 14680064 | tf_op jit(solution)/shard_map/ktqr,qkp->rtp/dot_general | solution.py:131
  415.8 52.2 %all_to_all.53 = f32[8,64,8,256]{3,1,2,0:T(8,128)S(1)} all-to-all(f32[8,64,8,256]{3,1,2,0:T(8,128)S(1)} %fusion.61), channel_id=1, replica_groups=mesh['az'=8,'col'=16] {'az'}, dimensions={0} | all-to-all | bytes 8388608 | tf_op jit(solution)/shard_map/all_to_all | solution.py:133
  468.0 4.4 copy.71
  (60 shorter events, 52.1 us)
Async XLA Ops:
  6.5 14.5 %collective-permute-start = (f32[64,64,1]{1,0,2:T(8,128)S(1)}, f32[64,64,1]{1,0,2:T(8,128)S(1)}, u32[]{:S(2)}, u32[]{:S(2)}) collective-permute-start(f32[64,64,1]{1,0,2:T(8,128)S(1)} %copy.80), channel_id=1, source_target_pairs={{0,16},{16,32},{32,48},{48,64},{64,80},{80,96},{96,112},{112,0},{1... | collective-permute-start | bytes 49160 | tf_op jit(solution)/shard_map/ppermute | solution.py:18
  8.9 7.6 %copy-start = (f32[64,64,256]{2,1,0:T(8,128)S(1)}, f32[64,64,256]{2,1,0:T(8,128)}, u32[]{:S(2)}) copy-start(f32[64,64,256]{2,1,0:T(8,128)} %param.5) | copy-start | bytes 12582916
  8.9 14.0 %collective-permute-start.1 = (f32[64,64,1]{1,0,2:T(8,128)S(1)}, f32[64,64,1]{1,0,2:T(8,128)S(1)}, u32[]{:S(2)}, u32[]{:S(2)}) collective-permute-start(f32[64,64,1]{1,0,2:T(8,128)S(1)} %copy.81), channel_id=1, source_target_pairs={{16,0},{32,16},{48,32},{64,48},{80,64},{96,80},{112,96},{0,112},{1... | collective-permute-start | bytes 49160 | tf_op jit(solution)/shard_map/ppermute | solution.py:21
  25.8 9.1 %copy-start.2 = (f32[64,64,256]{2,0,1:T(8,128)S(1)}, f32[64,64,256]{2,0,1:T(8,128)}, u32[]{:S(2)}) copy-start(f32[64,64,256]{2,0,1:T(8,128)} %copy.50) | copy-start | bytes 12582916
  25.8 9.1 %copy-start.3 = (f32[64,64,1]{2,0,1:T(8,128)S(1)}, f32[64,64,1]{2,0,1:T(8,128)}, u32[]{:S(2)}) copy-start(f32[64,64,1]{2,0,1:T(8,128)} %copy.48) | copy-start | bytes 49156
  27.0 7.7 %collective-permute-start.2 = (f32[64,1,258]{2,0,1:T(8,128)S(1)}, f32[64,1,258]{2,0,1:T(8,128)S(1)}, u32[]{:S(2)}, u32[]{:S(2)}) collective-permute-start(f32[64,1,258]{2,0,1:T(8,128)S(1)} %get-tuple-element.5), channel_id=1, source_target_pairs={{0,1},{1,2},{2,3},{3,4},{4,5},{5,6},{6,7},{7,8},{8,9},{9,10},{10,1... | collective-permute-start | bytes 198152 | tf_op jit(solution)/shard_map/ppermute | solution.py:18
  27.1 7.8 %collective-permute-start.3 = (f32[64,1,258]{2,0,1:T(8,128)S(1)}, f32[64,1,258]{2,0,1:T(8,128)S(1)}, u32[]{:S(2)}, u32[]{:S(2)}) collective-permute-start(f32[64,1,258]{2,0,1:T(8,128)S(1)} %get-tuple-element.6), channel_id=1, source_target_pairs={{1,0},{2,1},{3,2},{4,3},{5,4},{6,5},{7,6},{8,7},{9,8},{10,9},{11,1... | collective-permute-start | bytes 198152 | tf_op jit(solution)/shard_map/ppermute | solution.py:21
  32.7 5.4 %copy-start.1 = (f32[64,64,256]{2,1,0:T(8,128)S(1)}, f32[64,64,256]{2,1,0:T(8,128)}, u32[]{:S(2)}) copy-start(f32[64,64,256]{2,1,0:T(8,128)} %param.5) | copy-start | bytes 12582916
  54.9 5.4 %copy-start.5 = (s32[128,4]{0,1:T(4,128)S(1)}, s32[128,4]{0,1:T(4,128)}, u32[]{:S(2)}) copy-start(s32[128,4]{0,1:T(4,128)} %param.7) | copy-start | bytes 6148
  54.9 98.6 %all-to-all-start = ((f32[2,64,64,256]{3,1,0,2:T(8,128)}), f32[2,64,64,256]{3,1,0,2:T(8,128)}, u32[]{:S(2)}, u32[]{:S(2)}) async-start(f32[2,64,64,256]{3,1,0,2:T(8,128)} %pad_maximum_fusion), calls=%async_computation | async-start | bytes 16777216 | tf_op jit(solution)/shard_map/all_to_all | solution.py:94
  217.0 93.4 %all-to-all-start.1 = ((f32[512,8,256]{2,1,0:T(8,128)}), f32[512,8,256]{2,1,0:T(8,128)}, u32[]{:S(2)}, u32[]{:S(2)}) async-start(f32[512,8,256]{2,1,0:T(8,128)} %copy.57), calls=%async_computation.1 | async-start | bytes 8388608 | tf_op jit(solution)/shard_map/all_to_all | solution.py:99
  313.1 2.2 copy-start.4
  355.3 36.3 %all-to-all-start.2 = ((f32[4,1024,128]{2,0,1:T(4,128)}), f32[4,1024,128]{2,0,1:T(4,128)S(1)}, u32[]{:S(2)}, u32[]{:S(2)}) async-start(f32[4,1024,128]{2,0,1:T(4,128)} %copy.67), calls=%async_computation.2 | async-start | bytes 4194304 | tf_op jit(solution)/shard_map/all_to_all | solution.py:128
